TPU v7x, 128 devices: a whole 4x4x4 slice. The times are simulated.
128 devices in a mesh: strip: 128 (over z, x, y, core).
Axes of the slice: x: 4, y: 4, z: 4, core: 2. Of those that a mesh axis runs over, the one named last changes fastest.
Arguments:
- state: float32 [4096, 4096], P('strip'), may hold values from -6 to 6
- noise: float32 [4096, 4096], P('strip'), may hold values from -6 to 6
- step: float32 [1], replicated, may hold values from 0.3 to 0.7
- field_scale: float32 [1], replicated, may hold values from 0.6 to 1.2
- wave_scale: float32 [1], replicated, may hold values from 4 to 8
- source: float32 [2048, 2048], P('strip'), may hold values from -6 to 6
- obs_cells: int32 [8192], replicated, may hold values from 0 to 4194303
- obs_values: float32 [8192], replicated, may hold values from -3 to 3
Outputs:
- log_perm: float32 [2048, 2048], P('strip')
- pressure: float32 [2048, 2048], P('strip')
- loglik: float32 [], replicated
Inputs may be any that keep to these rules, and one draw needn't show every extreme that they name: `obs_cells`: each entry is row * 2048 + column of an observed cell of the field grid.
All inputs are finite; a program needn't handle non-finite values.
Results may differ from a plain program's by a relative error of at most 0.00011.
Values sent between devices are 32-bit elements; how exact they have to be, the bound alone decides.
A program may use at most 64 MiB of HBM per device.

v0:
```python
import functools
import math

import jax
import jax.numpy as jnp
import ml_dtypes
import numpy as np
from jax import lax
from jax.experimental import pallas as pl
from jax.experimental.pallas import tpu as pltpu
from jax.sharding import PartitionSpec as P

M = 4096
N = 2048
DEVICES = 128
ROWS = M // DEVICES
FIELD = N // DEVICES
KS = 72
ARRIVALS = ((0, 2), (2, 4))
DEPARTURES = ((0, 2), (2, 4))
AXIS = "strip"
MESH = pl.DeviceIdType.MESH
F32 = jnp.float32
BF16 = jnp.bfloat16


def halves(table):
    table = table.astype(np.float32)
    high = table.astype(ml_dtypes.bfloat16)
    low = (table - high.astype(np.float32)).astype(ml_dtypes.bfloat16)
    return np.stack([high, low])


def tables():
    b = np.arange(256)
    kl = np.arange(128)
    angle = 2 * np.pi * np.outer(kl, b) / 256
    top = np.zeros((16, 512))
    top[0, :256] = (-1.0) ** b
    row_forward = np.concatenate(
        [
            np.concatenate([np.cos(angle), np.sin(angle)], 1),
            np.concatenate([-np.sin(angle), np.cos(angle)], 1),
            top,
        ]
    )
    row_back = np.concatenate(
        [
            np.concatenate([np.cos(angle), np.sin(angle)], 1),
            np.concatenate([-np.sin(angle), np.cos(angle)], 1),
        ]
    )
    kv = np.arange(16)
    turn = 2 * np.pi * np.outer(kv, b) / M
    row_turn = np.stack([np.cos(turn), np.sin(turn)])
    ks = np.arange(KS)
    real = ks <= 64
    src = np.arange(DEVICES)
    angle = 2 * np.pi * np.outer(ks, src) / 128
    col_forward = np.concatenate([np.cos(angle), -np.sin(angle)]) * np.tile(real, 2)[:, None]
    weight = np.where((ks == 0) | (ks == 64), 1.0, 2.0) * real
    angle = angle.T[:64]
    col_back = np.concatenate([np.cos(angle) * weight, -np.sin(angle) * weight], 1)
    r = np.arange(32)
    lanes_in = [(v, q) for v in range(4) for q in range(32)]
    lanes_out = [(v, h * 8 + q) for h in range(4) for v in range(4) for q in range(8)]
    turn = 2 * np.pi * np.outer(ks, [q for _, q in lanes_in]) / M
    turn_back = 2 * np.pi * np.outer(ks, [q for _, q in lanes_out]) / M
    col_turn = np.stack([np.cos(turn), np.sin(turn), np.cos(turn_back), np.sin(turn_back)])
    vi, qi = np.array(lanes_in).T
    vo, qo = np.array(lanes_out).T
    same = vi[:, None] == vi[None, :]
    angle = 2 * np.pi * qi[:, None] * qi[None, :] / 32
    c, s = np.cos(angle) * same, np.sin(angle) * same
    mid_forward = np.block([[c, -s], [s, c]])
    same = vi[:, None] == vo[None, :]
    angle = 2 * np.pi * qi[:, None] * qo[None, :] / 32
    c, s = np.cos(angle) * same, np.sin(angle) * same
    mid_back = np.block([[c, s], [-s, c]])
    return (
        halves(row_forward),
        halves(row_back),
        row_turn.astype(np.float32),
        halves(col_forward),
        np.concatenate([halves(col_back)[k] for k in (0, 0, 1)], axis=1),
        col_turn.astype(np.float32),
        halves(mid_forward),
        halves(mid_back),
    )


def split(x):
    high = x.astype(BF16)
    return high, (x - high.astype(F32)).astype(BF16)


NN = (((1,), (0,)), ((), ()))
NT = (((1,), (1,)), ((), ()))


def product(left, right, form):
    (lh, ll), (rh, rl) = left, right
    axis_left, axis_right = form[0][0][0], form[0][1][0]
    return lax.dot_general(
        jnp.concatenate([lh, lh, ll], axis=axis_left),
        jnp.concatenate([rh, rl, rh], axis=axis_right),
        dimension_numbers=form,
        preferred_element_type=F32,
    )


def scaled(x, factor):
    if abs(factor) < 1e-12:
        return None
    if abs(factor - 1) < 1e-12:
        return x
    if abs(factor + 1) < 1e-12:
        return -x
    return x * F32(factor)


def plus(a, b):
    return b if a is None else a if b is None else a + b


def minus(a, b):
    if b is None:
        return a
    return -b if a is None else a - b


def turned(z, cos, sin):
    re, im = z
    out_re = scaled(re, cos) if re is not None else None
    out_im = scaled(re, sin) if re is not None else None
    if im is not None:
        out_re = minus(out_re, scaled(im, sin))
        out_im = plus(out_im, scaled(im, cos))
    return out_re, out_im


def added(a, b):
    return plus(a[0], b[0]), plus(a[1], b[1])


def less(a, b):
    return minus(a[0], b[0]), minus(a[1], b[1])


def real_dft(xs):
    count = len(xs)
    if count == 1:
        return [(xs[0], None)]
    even, odd = real_dft(xs[::2]), real_dft(xs[1::2])
    out = [None] * (count // 2 + 1)
    if count == 2:
        return [added(even[0], odd[0]), less(even[0], odd[0])]
    for k in range(count // 4 + 1):
        angle = -2 * math.pi * k / count
        t = turned(odd[k], math.cos(angle), math.sin(angle))
        out[k] = added(even[k], t)
        if k != count // 4:
            re, im = less(even[k], t)
            out[count // 2 - k] = (re, None if im is None else -im)
    return out


def back_dft(zs):
    count = len(zs)
    if count == 1:
        return list(zs)
    even, odd = back_dft(zs[::2]), back_dft(zs[1::2])
    out = [None] * count
    for k in range(count // 2):
        angle = 2 * math.pi * k / count
        t = turned(odd[k], math.cos(angle), math.sin(angle))
        out[k] = added(even[k], t)
        out[k + count // 2] = less(even[k], t)
    return out


def back_dft_real_first_half(zs):
    count = len(zs)
    even, odd = back_dft(zs[::2]), back_dft(zs[1::2])
    out = []
    for k in range(count // 2):
        angle = 2 * math.pi * k / count
        out.append(even[k][0] + turned(odd[k], math.cos(angle), math.sin(angle))[0])
    return out


def others_far_first(me):
    core, y, x, z = me % 2, (me // 2) % 4, (me // 8) % 4, me // 32
    cores = [core, 1 - core]
    ys = [2 * ((y + i) % 4) for i in range(4)]
    xs = [8 * ((x + i) % 4) for i in range(4)]
    zs = [32 * ((z + i) % 4) for i in range(4)]
    hops = (0, 1, 2, 1)
    offsets = [(a, b, c, d) for a in range(4) for b in range(4) for c in range(4) for d in range(2)][1:]
    offsets.sort(key=lambda o: (-(hops[o[0]] + hops[o[1]] + hops[o[2]]), (37 * o[0] + 17 * o[1] + 11 * o[2] + 5 * o[3]) % 13))
    return [(zs[a] + xs[b]) + (ys[c] + cores[d]) for a, b, c, d in offsets]


def send_to_all(me, others, piece, landing, send_sem, recv_sem):
    for other in others(me):
        pltpu.make_async_remote_copy(
            src_ref=piece(other),
            dst_ref=landing(me),
            send_sem=send_sem,
            recv_sem=recv_sem,
            device_id=(other,),
            device_id_type=MESH,
        ).start()


def wait_for_all(me, whole, send_sem, recv_sem):
    pltpu.make_async_remote_copy(
        src_ref=whole,
        dst_ref=whole,
        send_sem=send_sem,
        recv_sem=recv_sem,
        device_id=(lax.rem(me + 1, DEVICES),),
        device_id_type=MESH,
    ).wait()


def greet_all(me):
    barrier = pltpu.get_barrier_semaphore()

    for other in others_far_first(me):
        pl.semaphore_signal(barrier, inc=1, device_id=(other,), device_id_type=MESH)


def meet_all():
    pl.semaphore_wait(pltpu.get_barrier_semaphore(), DEVICES - 1)


def rows_forward(rate, state, noise, row_turn, z_high, z_low, row_forward, out):
    keep = jnp.sqrt(1.0 - rate * rate)
    for g in range(ROWS // 16):
        rows = slice(16 * g, 16 * g + 16)
        for h in range(2):
            xs = []
            for a in range(16):
                cols = slice(256 * a + 128 * h, 256 * a + 128 * h + 128)
                xs.append(keep * state[rows, cols] + rate * noise[rows, cols])
            ys = real_dft(xs)
            for kv in range(16):
                re, im = ys[kv] if kv <= 8 else ys[16 - kv]
                cos = row_turn[0, kv : kv + 1, 128 * h : 128 * h + 128]
                sin = row_turn[1, kv : kv + 1, 128 * h : 128 * h + 128]
                if kv > 8:
                    im = -im
                if kv == 0:
                    zr, zi = re, jnp.zeros_like(re)
                elif im is None:
                    zr, zi = re * cos, -(re * sin)
                else:
                    zr, zi = re * cos + im * sin, im * cos - re * sin
                spot = slice(kv * ROWS + 16 * g, kv * ROWS + 16 * g + 16)
                for part, lane in ((zr, 128 * h), (zi, 256 + 128 * h)):
                    high, low = split(part)
                    z_high[spot, lane : lane + 128] = high
                    z_low[spot, lane : lane + 128] = low
    for pair in range(2):
        rows = slice(256 * pair, 256 * pair + 256)
        res = product((row_forward[0], row_forward[1]), (z_high[rows, :], z_low[rows, :]), NT)
        for i in range(2):
            t = 2 * pair + i
            lanes = slice(128 * i, 128 * i + 128)
            im = res[128:256, lanes]
            if t == 0:
                first = (lax.broadcasted_iota(jnp.int32, (128, 128), 0) == 0) & (
                    lax.broadcasted_iota(jnp.int32, (128, 128), 1) < ROWS
                )
                im = jnp.where(first, jnp.broadcast_to(res[256:257, lanes], (128, 128)), im)
            out[pl.ds(t, 128, stride=8), :] = res[:128, lanes]
            out[pl.ds(4 + t, 128, stride=8), :] = im


def amplitudes(me, sigma, wave, amp):
    ks = lax.broadcasted_iota(jnp.int32, (KS, 128), 0)
    lane = lax.broadcasted_iota(jnp.int32, (KS, 128), 1)
    k0 = ks + 128 * (lane % 32)
    q0 = jnp.minimum(k0, M - k0).astype(F32)
    base = q0 * q0 + wave * wave
    gain = sigma * wave * F32(2.0 / (math.sqrt(math.pi) * M))
    for v in range(4):
        k1 = 16 * me + 4 * v + lane // 32
        q1 = k1.astype(F32)
        value = gain / (base + q1 * q1)
        if v == 0:
            alone = k1 == 0
            value = jnp.where(alone, 0.5 * value, value)
            top = jnp.where(alone, 0.5 * gain / (base + F32(N) * F32(N)), value)
            amp[4] = top
        else:
            amp[4 + v] = value
        amp[v] = value


def columns(first, last, got, amp, col_forward, col_back, col_turn, mid_forward, mid_back, out):
    tiles = list(range(2 * first, 2 * last))
    pieces = jnp.concatenate([got[pl.ds(t, 128, stride=8), :] for t in tiles], axis=1)
    spec = product((col_forward[0], col_forward[1]), split(pieces), NN)
    parts = []
    for i in range(len(tiles)):
        lanes = slice(128 * i, 128 * i + 128)
        re, im = spec[:KS, lanes], spec[KS:, lanes]
        cos, sin = col_turn[0], col_turn[1]
        parts.append(jnp.concatenate([re * cos + im * sin, im * cos - re * sin], axis=1))
    full = product(split(jnp.concatenate(parts, axis=0)), (mid_forward[0], mid_forward[1]), NN)
    factor = jnp.concatenate([amp[t] for t in tiles], axis=0)
    full = full * jnp.concatenate([factor, factor], axis=1)
    back = product(split(full), (mid_back[0], mid_back[1]), NN)
    sides = []
    for i in range(len(tiles)):
        rows = slice(KS * i, KS * i + KS)
        re, im = back[rows, :128], back[rows, 128:]
        cos, sin = col_turn[2], col_turn[3]
        sides.append(jnp.concatenate([re * cos - im * sin, im * cos + re * sin], axis=0))
    high, low = split(jnp.concatenate(sides, axis=1))
    field = lax.dot_general(col_back[...], jnp.concatenate([high, low, high], axis=0), NN, preferred_element_type=F32)
    lane = lax.broadcasted_iota(jnp.int32, (64, 128), 1)
    for i, t in enumerate(tiles):
        here = field[:, 128 * i : 128 * i + 128]
        later, sooner = pltpu.roll(here, 32, 1), pltpu.roll(here, 96, 1)
        out[pl.ds(t, 64, stride=16), :] = jnp.where(lane < 32, pltpu.roll(later, 1, 0), later)
        out[pl.ds(8 + t, 64, stride=16), :] = jnp.where(lane >= 96, pltpu.roll(sooner, 63, 0), sooner)


def rows_back(got, row_back, row_turn, put):
    blocks = [got[pl.ds(t, 128, stride=8), :].T for t in range(8)]
    row = lax.broadcasted_iota(jnp.int32, (128, 128), 0)
    lane = lax.broadcasted_iota(jnp.int32, (128, 128), 1)
    sign = (1 - 2 * (lane[:8] % 2)).astype(F32)
    tops = [jnp.broadcast_to(blocks[4][32 * g : 32 * g + 8, :1], (8, 128)) * sign for g in range(4)]
    blocks[4] = jnp.where((row % 32 < 8) & (lane == 0), 0.0, blocks[4])
    sides = jnp.concatenate([jnp.concatenate(blocks[:4], axis=0), jnp.concatenate(blocks[4:], axis=0)], axis=1)
    q = product(split(sides), (row_back[0], row_back[1]), NN)
    for h in range(2):
        for g in range(4):
            zs = []
            for kv in range(16):
                at = 128 * (kv // 4) + 32 * g + 8 * (kv % 4)
                rows = slice(at, at + 8)
                zr, zi = q[rows, 128 * h : 128 * h + 128], q[rows, 256 + 128 * h : 384 + 128 * h]
                cos = row_turn[0, kv : kv + 1, 128 * h : 128 * h + 128]
                sin = row_turn[1, kv : kv + 1, 128 * h : 128 * h + 128]
                zs.append((zr, zi) if kv == 0 else (zr * cos - zi * sin, zi * cos + zr * sin))
            for a, value in enumerate(back_dft_real_first_half(zs)):
                put(8 * g, 256 * a + 128 * h, value + tops[g])


def gather_observations(me, cells, values, counts, means, hot, parts):
    counts[...] = jnp.zeros_like(counts)

    @pl.loop(0, 8)
    def _(c):
        for i in range(8):
            cell = cells[pl.ds(8 * c + i, 1), :]
            value = values[pl.ds(8 * c + i, 1), :]
            row = cell // N - FIELD * me
            col = cell % N
            inside = (row >= 0) & (row < FIELD)
            spot = jnp.where(inside, (row // 8) * 128 + (col // 128) * 8 + row % 8, -1)
            lane = jnp.where(inside, col % 128, -1)
            lanes = slice(128 * i, 128 * i + 128)
            here = lax.broadcasted_iota(jnp.int32, (256, 128), 0) == spot
            hot[c, :, lanes] = jnp.where(here, 1.0, 0.0).astype(BF16)
            there = lax.broadcasted_iota(jnp.int32, (128, 128), 0) == lane
            high = value.astype(BF16).astype(F32)
            middle = (value - high).astype(BF16).astype(F32)
            low = value - high - middle
            for j, piece in enumerate((jnp.ones_like(value), high, middle, low)):
                parts[128 * j : 128 * j + 128, lanes] = jnp.where(there, piece, 0.0).astype(BF16)
        counts[...] += lax.dot_general(hot[c], parts[...], NT, preferred_element_type=F32)

    number = counts[:, :128]
    total = counts[:, 128:256] + counts[:, 256:384] + counts[:, 384:]
    means[...] = total / jnp.maximum(number, 1.0)


def spread_observations(me, cells, values, means, hot, spread):
    turned_means = jnp.concatenate([means[:128, :].T, means[128:, :].T], axis=1)
    pieces = jnp.concatenate(split(turned_means), axis=0)
    spread[...] = jnp.zeros_like(spread)

    @pl.loop(0, 8)
    def _(c):
        totals = [jnp.zeros((8, 128), F32) for _ in range(4)]
        for b in range(4):
            picked = jnp.dot(pieces, hot[c, :, 256 * b : 256 * b + 256], preferred_element_type=F32)
            for i in range(2):
                cell = cells[pl.ds(8 * c + 2 * b + i, 1), :]
                value = values[pl.ds(8 * c + 2 * b + i, 1), :]
                row = cell // N - FIELD * me
                lane = jnp.where((row >= 0) & (row < FIELD), cell % 128, -1)
                lanes = slice(128 * i, 128 * i + 128)
                mean = picked[:128, lanes] + picked[128:, lanes]
                there = lax.broadcasted_iota(jnp.int32, (128, 128), 0) == lane
                off = jnp.where(there, value - mean, 0.0)
                off = off * off
                for k in range(16):
                    totals[k % 4] = totals[k % 4] + off[8 * k : 8 * k + 8]
        spread[...] += (totals[0] + totals[1]) + (totals[2] + totals[3])


def exchange_edges(me, own_low, own_high, ext, sems):
    up, down = lax.rem(me + 1, DEVICES), lax.rem(me + DEVICES - 1, DEVICES)
    return [
        pltpu.make_async_remote_copy(
            src_ref=own_low, dst_ref=ext.at[pl.ds(24, 8), :], send_sem=sems.at[0], recv_sem=sems.at[1],
            device_id=(down,), device_id_type=MESH,
        ),
        pltpu.make_async_remote_copy(
            src_ref=own_high, dst_ref=ext.at[pl.ds(0, 8), :], send_sem=sems.at[2], recv_sem=sems.at[3],
            device_id=(up,), device_id_type=MESH,
        ),
    ]


TILES = N // 128
OWN = slice(8, 24)


def tile(j):
    return slice(128 * j, 128 * j + 128)


def neighbours(load):
    lane = lax.broadcasted_iota(jnp.int32, (32, 128), 1)
    values = [load(0), load(1)]
    rights = [pltpu.roll(v, 1, 1) for v in values]
    lefts = [pltpu.roll(v, 127, 1) for v in values]
    before = jnp.zeros_like(rights[0])
    for j in range(TILES):
        if j == TILES - 1:
            after = jnp.zeros_like(before)
        else:
            after = lefts[1]
        west = jnp.where(lane == 0, before, rights[0])
        east = jnp.where(lane == 127, after, lefts[0])
        north = pltpu.roll(values[0], 1, 0)
        south = pltpu.roll(values[0], 31, 0)
        yield j, values[0], north, south, west, east
        before = rights[0]
        if j + 1 < TILES:
            values = values[1:]
            rights = rights[1:]
            lefts = lefts[1:]
            if j + 2 < TILES:
                values.append(load(j + 2))
                rights.append(pltpu.roll(values[1], 1, 1))
                lefts.append(pltpu.roll(values[1], 127, 1))


def krylov(me, lx, sx, kappa, coefs, diag, v0, z0, z1, z2):
    row = lax.broadcasted_iota(jnp.int32, (32, 128), 0)
    lane = lax.broadcasted_iota(jnp.int32, (32, 128), 1)
    valid = ((row >= 8) | (me > 0)) & ((row < 24) | (me < DEVICES - 1))
    for j in range(TILES):
        kappa[:, tile(j)] = jnp.where(valid, jnp.exp(lx[:, tile(j)]), 0.0)
    sums = [jnp.zeros((16, 128), F32) for _ in range(8)]
    for j, k, kn, ks, kw, ke in neighbours(lambda j: kappa[:, tile(j)]):
        north, south, west, east = 0.5 * (k + kn), 0.5 * (k + ks), 0.5 * (k + kw), 0.5 * (k + ke)
        d = north + south + west + east
        inverse = jnp.where(valid, 1.0 / d, 0.0)
        coefs[0, :, tile(j)] = north * inverse
        coefs[1, :, tile(j)] = south * inverse
        coefs[2, :, tile(j)] = west * inverse
        coefs[3, :, tile(j)] = east * inverse
        source = sx[:, tile(j)]
        first = source * inverse
        diag[:, tile(j)] = d[OWN]
        v0[:, tile(j)] = first
        sums[0] = sums[0] + source[OWN] * first[OWN]

    def beside(values):
        for j, v, vn, vs, vw, ve in neighbours(lambda j: values[:, tile(j)]):
            yield j, v, (coefs[0, :, tile(j)] * vn + coefs[1, :, tile(j)] * vs) + (
                coefs[2, :, tile(j)] * vw + coefs[3, :, tile(j)] * ve
            )

    for j, v, s in beside(v0):
        z = v - s
        z0[:, tile(j)] = z
        own = z[OWN]
        sums[1] = sums[1] + sx[OWN, tile(j)] * own
        sums[2] = sums[2] + diag[:, tile(j)] * own * own
    for j, v, s in beside(z0):
        z = -s
        z1[:, tile(j)] = z
        own = diag[:, tile(j)] * z[OWN]
        sums[3] = sums[3] + own * v[OWN]
        sums[4] = sums[4] + own * z[OWN]
    for j, v, s in beside(z1):
        z = -2.0 * s - z0[:, tile(j)]
        z2[:, tile(j)] = z
        own = diag[:, tile(j)] * z[OWN]
        sums[5] = sums[5] + own * v[OWN]
        sums[6] = sums[6] + own * z[OWN]
    for j, v, s in beside(z2):
        z = -2.0 * s[OWN] - z1[OWN, tile(j)]
        sums[7] = sums[7] + diag[:, tile(j)] * v[OWN] * z
    return sums


def lane_totals(sums):
    count = len(sums)
    high = -(-count // 8) * 8
    rows = [jnp.sum(s, axis=0, keepdims=True) for s in sums] + [jnp.zeros((1, 128), F32)] * (high - count)
    rows = jnp.concatenate(rows, axis=0)
    totals = jnp.broadcast_to(jnp.sum(rows, axis=1, keepdims=True), (high, 128))
    at = lax.broadcasted_iota(jnp.int32, (high, 128), 0) == lax.broadcasted_iota(jnp.int32, (high, 128), 1)
    return jnp.sum(jnp.where(at, totals, 0.0), axis=0, keepdims=True)


def share(me, row, mine, all_rows, sems):
    mine[0:1, :] = row
    all_rows[pl.ds(me, 1), :] = row
    send_to_all(me, others_far_first, lambda d: mine.at[pl.ds(0, 1), :], lambda s: all_rows.at[pl.ds(s, 1), :], sems.at[0], sems.at[1])


def shared(me, all_rows, sems):
    wait_for_all(me, all_rows.at[pl.ds(0, DEVICES - 1), :], sems.at[0], sems.at[1])


PAIRS = [(i, j) for i in range(4) for j in range(i, 4)]


def misfit_parts(guess, fields, counts, means, spread):
    sums = [spread[...]] + [jnp.zeros((8, 128), F32) for _ in range(14)]
    for j in range(TILES):
        for g in range(2):
            rows = slice(128 * g + 8 * j, 128 * g + 8 * j + 8)
            us = [f[8 + 8 * g : 16 + 8 * g, tile(j)] for f in fields]
            n = counts[rows, :128]
            off = ((guess[0] * us[0] + guess[1] * us[1]) + (guess[2] * us[2] + guess[3] * us[3])) - means[rows, :]
            many = n * off
            sums[0] = sums[0] + many * off
            for i in range(4):
                sums[1 + i] = sums[1 + i] + many * us[i]
            scaled_us = [n * u for u in us]
            for k, (i, l) in enumerate(PAIRS):
                sums[5 + k] = sums[5 + k] + scaled_us[i] * us[l]
    row = lane_totals(sums)
    lane = lax.broadcasted_iota(jnp.int32, (1, 128), 1)
    for i in range(4):
        row = jnp.where(lane == 15 + i, guess[i][:1], row)
    return pltpu.roll(jnp.broadcast_to(row, (8, 128)), 8, 1)[:1]


def misfit(y, rows):
    table = rows.T[8:]
    off = [y[i][:1] - table[15 + i : 16 + i] for i in range(4)]
    total = table[0:1]
    for i in range(4):
        total = total + 2.0 * off[i] * table[1 + i : 2 + i]
    for k, (i, l) in enumerate(PAIRS):
        term = off[i] * off[l] * table[5 + k : 6 + k]
        total = total + (term if i == l else 2.0 * term)
    return jnp.sum(total)


def pair_sum(x, y):
    total = x[0] + y[0]
    step = total - x[0]
    rest = (x[0] - (total - step)) + (y[0] - step)
    rest = rest + (x[1] + y[1])
    high = total + rest
    return high, rest - (high - total)


def pair_scaled(x, factor):
    return x[0] * F32(factor), x[1] * F32(factor)


def pair_total(rows):
    zero = jnp.zeros((8, 128), F32)
    terms = [(rows[8 * k : 8 * k + 8], zero) for k in range(DEVICES // 8)]
    while len(terms) > 1:
        terms = [pair_sum(terms[2 * k], terms[2 * k + 1]) for k in range(len(terms) // 2)]
    total = terms[0]
    for shift in (4, 2, 1):
        total = pair_sum(total, (pltpu.roll(total[0], shift, 0), pltpu.roll(total[1], shift, 0)))
    return total


def cut(a):
    t = F32(4097.0) * a
    high = t - (t - a)
    return high, a - high


def system(take, scale, add):
    g0, e0, m0, m1, q11, q12, q22, q23 = take

    def less(a, b):
        return add(a, scale(b, -1.0))

    m = [m0, m1, less(scale(q11, 2.0), m0), less(scale(q12, 2.0), m1), less(scale(q22, 2.0), m0), less(scale(q23, 2.0), m1)]

    def inner(i, j):
        return scale(add(m[i + j], m[abs(i - j)]), 0.5)

    def energy(i, j):
        return add(inner(i, j), scale(add(inner(i, j + 1), inner(i, abs(j - 1))), 0.5))

    gram = [[None] * 4 for _ in range(4)]
    gram[0][0] = e0
    for j in range(3):
        gram[j + 1][0] = inner(0, j)
        for i in range(j + 1):
            gram[j + 1][i + 1] = energy(i, j)
    tail = less(m0, e0)
    return gram, [g0, e0, tail, less(scale(less(m1, tail), 2.0), e0)]


def lanes_of(row):
    return [jnp.broadcast_to(row[:1, i : i + 1], (8, 128)) for i in range(8)]


def solver(gram):
    gram = [list(r) for r in gram]
    factors = [[None] * 4 for _ in range(4)]
    inverse = []
    whole = [gram[i][i] for i in range(4)]
    for k in range(4):
        pivot = gram[k][k]
        inverse.append(jnp.where(pivot > 1e-6 * whole[k], 1.0 / pivot, 0.0))
        for i in range(k + 1, 4):
            factors[i][k] = gram[i][k] * inverse[k]
        for i in range(k + 1, 4):
            for j in range(k + 1, i + 1):
                gram[i][j] = gram[i][j] - factors[i][k] * gram[j][k]

    def solve(right):
        right = list(right)
        for k in range(4):
            for i in range(k + 1, 4):
                right[i] = right[i] - factors[i][k] * right[k]
        out = [right[k] * inverse[k] for k in range(4)]
        for k in (2, 1, 0):
            for i in range(k + 1, 4):
                out[k] = out[k] - factors[i][k] * out[i]
        return out

    return solve


def weights(row):
    gram, right = system(lanes_of(row), lambda a, f: a * F32(f), lambda a, b: a + b)
    return solver(gram)(right)


def refined_weights(total):
    gram, right = system(list(zip(lanes_of(total[0]), lanes_of(total[1]))), pair_scaled, pair_sum)
    solve = solver([[g and g[0] for g in r] for r in gram])
    y = solve([r[0] for r in right])
    y_cut = [cut(v) for v in y]
    cuts = [[g and cut(g[0]) for g in r] for r in gram]
    left = []
    for i in range(4):
        rest = right[i]
        for j in range(4):
            a, b = max(i, j), min(i, j)
            high, low = gram[a][b]
            (gh, gl), (yh, yl) = cuts[a][b], y_cut[j]
            main = high * y[j]
            error = ((gh * yh - main) + (gh * yl + gl * yh)) + gl * yl
            rest = pair_sum(rest, (-main, -(error + low * y[j])))
        left.append(rest[0] + rest[1])
    better = [v + d for v, d in zip(y, solve(left))]
    size = jnp.maximum(jnp.maximum(jnp.abs(y[0]), jnp.abs(y[1])), jnp.maximum(jnp.abs(y[2]), jnp.abs(y[3])))
    close = jnp.abs(better[0] - y[0]) <= 0.01 * size
    for k in range(1, 4):
        close = close & (jnp.abs(better[k] - y[k]) <= 0.01 * size)
    return [jnp.where(close, b, v) for b, v in zip(better, y)]


LOADS = ("state", "noise", "source", "cells", "values",
         "row_forward", "row_back", "row_turn", "col_forward", "col_back", "col_turn", "mid_forward", "mid_back")


def kernel(*refs):
    (step, sigma, wave), refs = refs[:3], refs[3:]
    count = len(LOADS)
    sources, refs = refs[:count], refs[count:]
    (log_perm_out, pressure_out, loglik), refs = refs[:3], refs[3:]
    held, refs = refs[:count], refs[count:]
    (
        z_high, z_low, sent1, got1, amp, sent2, got2,
        counts, means, hot, parts, spread,
        lx, sx, kappa, coefs, diag, v0, z0, z1, z2, mine, everyone, pressure, sems, load_sems, edge_sems, end_sems,
    ) = refs
    me = lax.axis_index(AXIS)
    loads = {
        name: pltpu.make_async_copy(sources[k], held[k], load_sems.at[k]) for k, name in enumerate(LOADS)
    }
    early = ("state", "noise", "row_turn", "row_forward")
    for name in early:
        loads[name].start()
    (state, noise, source, cells, values,
     row_forward, row_back, row_turn, col_forward, col_back, col_turn, mid_forward, mid_back) = held
    greet_all(me)
    for name in early:
        loads[name].wait()
    for name in LOADS:
        if name not in early:
            loads[name].start()
    rows_forward(step[0], state, noise, row_turn, z_high, z_low, row_forward, sent1)
    loads["source"].wait()
    meet_all()
    for part, (first, last) in enumerate(ARRIVALS):
        size = 2 * (last - first)
        send_to_all(
            me, others_far_first, lambda d: sent1.at[pl.ds(8 * d + 2 * first, size), :],
            lambda s: got1.at[pl.ds(8 * s + 2 * first, size), :], sems.at[2 * part], sems.at[2 * part + 1],
        )
    source_edges = exchange_edges(me, source.at[pl.ds(0, 8), :], source.at[pl.ds(8, 8), :], sx, edge_sems)
    for copy in source_edges:
        copy.start()
    own = pl.ds(pl.multiple_of(8 * me, 8), 8)
    got1[own, :] = sent1[own, :]
    sx[OWN, :] = source[...]
    amplitudes(me, sigma[0], wave[0], amp)
    for name in ("col_forward", "col_back", "col_turn", "mid_forward", "mid_back", "row_back", "cells", "values"):
        loads[name].wait()
    gather_observations(me, cells, values, counts, means, hot, parts)
    ready = 0
    for part, (first, last) in enumerate(DEPARTURES):
        while ready < len(ARRIVALS) and ARRIVALS[ready][0] < last:
            size = 2 * (ARRIVALS[ready][1] - ARRIVALS[ready][0])
            wait_for_all(me, got1.at[pl.ds(0, size * (DEVICES - 1)), :], sems.at[2 * ready], sems.at[2 * ready + 1])
            ready += 1
        columns(first, last, got1, amp, col_forward, col_back, col_turn, mid_forward, mid_back, sent2)
        size = 2 * (last - first)
        send_to_all(
            me, others_far_first, lambda d: sent2.at[pl.ds(8 * d + 2 * first, size), :],
            lambda s: got2.at[pl.ds(8 * s + 2 * first, size), :], sems.at[8 + 2 * part], sems.at[9 + 2 * part],
        )
    got2[own, :] = sent2[own, :]
    spread_observations(me, cells, values, means, hot, spread)
    for part, (first, last) in enumerate(DEPARTURES):
        size = 2 * (last - first)
        wait_for_all(me, got2.at[pl.ds(0, size * (DEVICES - 1)), :], sems.at[8 + 2 * part], sems.at[9 + 2 * part])

    def put(row, at, value):
        lx[row : row + 8, at : at + 128] = value

    rows_back(got2, row_back, row_turn, put)
    write = pltpu.make_async_copy(lx.at[pl.ds(8, FIELD), :], log_perm_out, load_sems.at[count])
    write.start()
    for copy in source_edges:
        copy.wait()
    sums = krylov(me, lx, sx, kappa, coefs, diag, v0, z0, z1, z2)
    row = lane_totals(sums)
    fields = (v0, z0, z1, z2)
    guess = weights(row)
    fine = jnp.abs(guess[0]) < 64.0
    for i in range(1, 4):
        fine = fine & (jnp.abs(guess[i]) < 64.0)
    guess = [jnp.where(fine, g, 0.0) for g in guess]
    share(me, row + misfit_parts(guess, fields, counts, means, spread), mine, everyone, end_sems)
    shared(me, everyone, end_sems)
    y = refined_weights(pair_total(everyone[...]))
    for j in range(TILES):
        for g in range(2):
            us = [f[8 + 8 * g : 16 + 8 * g, tile(j)] for f in fields]
            pressure[8 * g : 8 * g + 8, tile(j)] = (y[0] * us[0] + y[1] * us[1]) + (y[2] * us[2] + y[3] * us[3])
    write_pressure = pltpu.make_async_copy(pressure, pressure_out, load_sems.at[count + 1])
    write_pressure.start()
    loglik[0, 0] = F32(-2.0 / 8192) * misfit(y, everyone[...])
    write.wait()
    write_pressure.wait()


def finish(log_perm, pressure, loglik, log_perm_out, pressure_out, loglik_out, sems):
    copies = [
        pltpu.make_async_copy(log_perm, log_perm_out, sems.at[0]),
        pltpu.make_async_copy(pressure, pressure_out, sems.at[1]),
    ]
    for copy in copies:
        copy.start()
    loglik_out[0, 0] = loglik[0, 0]
    for copy in copies:
        copy.wait()


def body(state, noise, step, field_scale, wave_scale, source, obs_cells, obs_values):
    anywhere = pl.BlockSpec(memory_space=pl.ANY)
    smem = pl.BlockSpec(memory_space=pltpu.SMEM)
    field = pltpu.VMEM((32, N), F32)
    own = pltpu.VMEM((FIELD, N), F32)
    arrays = [state, noise, source, obs_cells.reshape(64, 128), obs_values.reshape(64, 128)]
    arrays += [jnp.asarray(t) for t in tables()]
    log_perm, pressure, loglik = pl.pallas_call(
        kernel,
        out_shape=(
            jax.ShapeDtypeStruct((FIELD, N), F32),
            jax.ShapeDtypeStruct((FIELD, N), F32),
            jax.ShapeDtypeStruct((1, 1), F32),
        ),
        in_specs=[pl.BlockSpec(memory_space=pltpu.SMEM)] * 3 + [anywhere] * len(arrays),
        out_specs=(anywhere, anywhere, smem),
        scratch_shapes=[
            pltpu.VMEM(a.shape, a.dtype) for a in arrays
        ] + [
            pltpu.VMEM((512, 512), BF16),
            pltpu.VMEM((512, 512), BF16),
            pltpu.VMEM((1024, 128), F32),
            pltpu.VMEM((1024, 128), F32),
            pltpu.VMEM((8, KS, 128), F32),
            pltpu.VMEM((1024, 128), F32),
            pltpu.VMEM((1024, 128), F32),
            pltpu.VMEM((256, 512), F32),
            pltpu.VMEM((256, 128), F32),
            pltpu.VMEM((8, 256, 1024), BF16),
            pltpu.VMEM((512, 1024), BF16),
            pltpu.VMEM((8, 128), F32),
            field,
            field,
            field,
            pltpu.VMEM((4, 32, N), F32),
            own,
            field,
            field,
            field,
            field,
            pltpu.VMEM((8, 128), F32),
            pltpu.VMEM((DEVICES, 128), F32),
            own,
            pltpu.SemaphoreType.DMA((16,)),
            pltpu.SemaphoreType.DMA((len(arrays) + 2,)),
            pltpu.SemaphoreType.DMA((4,)),
            pltpu.SemaphoreType.DMA((2,)),
        ],
        compiler_params=pltpu.CompilerParams(collective_id=0, has_side_effects=True, vmem_limit_bytes=40 * 2**20),
    )(step, field_scale, wave_scale, *[pltpu.with_memory_space_constraint(a, pltpu.HBM) for a in arrays])
    log_perm, pressure, loglik = pl.pallas_call(
        finish,
        out_shape=(
            jax.ShapeDtypeStruct((FIELD, N), F32),
            jax.ShapeDtypeStruct((FIELD, N), F32),
            jax.ShapeDtypeStruct((1, 1), F32),
        ),
        in_specs=[anywhere, anywhere, smem],
        out_specs=(anywhere, anywhere, smem),
        scratch_shapes=[pltpu.SemaphoreType.DMA((2,))],
        compiler_params=pltpu.CompilerParams(vmem_limit_bytes=2**20),
    )(log_perm, pressure, loglik)
    return log_perm, pressure, loglik.reshape(())


def solution(mesh):
    in_specs = (P(AXIS, None), P(AXIS, None), P(), P(), P(), P(AXIS, None), P(), P())
    out_specs = (P(AXIS, None), P(AXIS, None), P())
    return jax.shard_map(body, mesh=mesh, in_specs=in_specs, out_specs=out_specs, check_vma=False)
```

profile of v0, /device:TPU:1, one launch (start us, length us, event | category | flops | bytes accessed | tf_op | source)
XLA Modules:
  0.0 43.0 jit_solution(2099834068770470190)
XLA Ops:
  2.6 38.6 %shard_map.175 = (f32[16,2048]{1,0:T(8,128)S(1)}, f32[16,2048]{1,0:T(8,128)S(1)}, f32[1,1]{1,0:T(1,128)}) custom-call(f32[1]{0:T(128)S(6)} %copy.19.refs_0_, f32[1]{0:T(128)S(6)} %copy.20.refs_1_, f32[1]{0:T(128)S(6)} %copy.21.refs_2_, f32[32,4096]{1,0:T(8,128)} %refs_3_.1, f32[32,4096]{1,0:T(8,128)} %refs_4_.1, f32[16,2048]{1,0:T(8,128)} %refs_5_.1, ...), custom_call_target="tpu_custom_call" | custom-call | tf_op jit(solution)/shard_map/pallas_call | solution.py:798
  41.1 1.9 %shard_map.176 = (f32[16,2048]{1,0:T(8,128)}, f32[16,2048]{1,0:T(8,128)}, f32[1,1]{1,0:T(1,128)}) custom-call(f32[16,2048]{1,0:T(8,128)S(1)} %get-tuple-element.9.log_perm, f32[16,2048]{1,0:T(8,128)S(1)} %get-tuple-element.10.pressure, f32[1,1]{1,0:T(1,128)} %get-tuple-element.11.loglik), custom_call_target="tpu_custom_call" | custom-call | tf_op jit(solution)/shard_map/pallas_call | solution.py:841
where the time goes:
time: 43.2 us; the launch traced here: 43 us
  Pallas kernels  40.4 us (94%)
  between operations  2.58 us (6%)
    pallas_call x1, Pallas kernels, body(): pl.pallas_call(kernel, out_shape=(jax.ShapeDtypeStruct((FIELD, N), F32),...  38.6 us
    pallas_call x1, Pallas kernels, body(): pl.pallas_call(finish, out_shape=(jax.ShapeDtypeStruct((FIELD, N), F32),...  1.86 us

commit v1 on v0

--- a/solution.py
+++ b/solution.py
@@ -329,15 +329,20 @@
         out[pl.ds(8 + t, 64, stride=16), :] = jnp.where(lane >= 96, pltpu.roll(sooner, 63, 0), sooner)
 
 
-def rows_back(got, row_back, row_turn, put):
-    blocks = [got[pl.ds(t, 128, stride=8), :].T for t in range(8)]
+def rows_back(got, row_back, row_turn, arrive, put):
+    arrive(0)
+    blocks = [got[pl.ds(t, 128, stride=8), :].T for t in range(4)]
+    re = split(jnp.concatenate(blocks, axis=0))
+    arrive(1)
+    blocks += [got[pl.ds(t, 128, stride=8), :].T for t in range(4, 8)]
     row = lax.broadcasted_iota(jnp.int32, (128, 128), 0)
     lane = lax.broadcasted_iota(jnp.int32, (128, 128), 1)
     sign = (1 - 2 * (lane[:8] % 2)).astype(F32)
     tops = [jnp.broadcast_to(blocks[4][32 * g : 32 * g + 8, :1], (8, 128)) * sign for g in range(4)]
     blocks[4] = jnp.where((row % 32 < 8) & (lane == 0), 0.0, blocks[4])
-    sides = jnp.concatenate([jnp.concatenate(blocks[:4], axis=0), jnp.concatenate(blocks[4:], axis=0)], axis=1)
-    q = product(split(sides), (row_back[0], row_back[1]), NN)
+    im = split(jnp.concatenate(blocks[4:], axis=0))
+    sides = [jnp.concatenate(pair, axis=1) for pair in zip(re, im)]
+    q = product(sides, (row_back[0], row_back[1]), NN)
     for h in range(2):
         for g in range(4):
             zs = []
@@ -742,14 +747,14 @@
         )
     got2[own, :] = sent2[own, :]
     spread_observations(me, cells, values, means, hot, spread)
-    for part, (first, last) in enumerate(DEPARTURES):
-        size = 2 * (last - first)
+    def arrive(part):
+        size = 2 * (DEPARTURES[part][1] - DEPARTURES[part][0])
         wait_for_all(me, got2.at[pl.ds(0, size * (DEVICES - 1)), :], sems.at[8 + 2 * part], sems.at[9 + 2 * part])
 
     def put(row, at, value):
         lx[row : row + 8, at : at + 128] = value
 
-    rows_back(got2, row_back, row_turn, put)
+    rows_back(got2, row_back, row_turn, arrive, put)
     write = pltpu.make_async_copy(lx.at[pl.ds(8, FIELD), :], log_perm_out, load_sems.at[count])
     write.start()
     for copy in source_edges:

time: 43.2 us -> 43.2 us (level)
  no operation moved by 1% of the time
where the time goes in v1:
time: 43.2 us; the launch traced here: 43 us
  Pallas kernels  40.4 us (94%)
  between operations  2.58 us (6%)
    pallas_call x1, Pallas kernels, body(): pl.pallas_call(kernel, out_shape=(jax.ShapeDtypeStruct((FIELD, N), F32),...  38.6 us
    pallas_call x1, Pallas kernels, body(): pl.pallas_call(finish, out_shape=(jax.ShapeDtypeStruct((FIELD, N), F32),...  1.86 us

profile of v1, /device:TPU:1, one launch (start us, length us, event | category | flops | bytes accessed | tf_op | source)
XLA Modules:
  0.0 43.0 jit_solution(6177919860515659813)
XLA Ops:
  2.6 38.6 %shard_map.175 = (f32[16,2048]{1,0:T(8,128)S(1)}, f32[16,2048]{1,0:T(8,128)S(1)}, f32[1,1]{1,0:T(1,128)}) custom-call(f32[1]{0:T(128)S(6)} %copy.19.refs_0_, f32[1]{0:T(128)S(6)} %copy.20.refs_1_, f32[1]{0:T(128)S(6)} %copy.21.refs_2_, f32[32,4096]{1,0:T(8,128)} %refs_3_.1, f32[32,4096]{1,0:T(8,128)} %refs_4_.1, f32[16,2048]{1,0:T(8,128)} %refs_5_.1, ...), custom_call_target="tpu_custom_call" | custom-call | tf_op jit(solution)/shard_map/pallas_call | solution.py:803
  41.1 1.9 %shard_map.176 = (f32[16,2048]{1,0:T(8,128)}, f32[16,2048]{1,0:T(8,128)}, f32[1,1]{1,0:T(1,128)}) custom-call(f32[16,2048]{1,0:T(8,128)S(1)} %get-tuple-element.9.log_perm, f32[16,2048]{1,0:T(8,128)S(1)} %get-tuple-element.10.pressure, f32[1,1]{1,0:T(1,128)} %get-tuple-element.11.loglik), custom_call_target="tpu_custom_call" | custom-call | tf_op jit(solution)/shard_map/pallas_call | solution.py:846
